TPU v7x, 32 devices: a whole 2x2x4 slice. The times are simulated.
32 devices in a mesh: band: 16 (over z, x, core), fld: 2 (over y).
Axes of the slice: x: 2, y: 2, z: 4, core: 2. Of those that a mesh axis runs over, the one named last changes fastest.
Arguments:
- grid_field: bfloat16 [2, 4, 1280, 2, 5248], P(None, 'fld', 'band'), may hold values from -6 to 6
- coupling: float32 [2, 4], P(None, 'fld'), may hold values from 0.1 to 1
- points: int32 [1280], replicated, may hold values from 20 to 5136, as said below
- lat_ids: int32 [1280], P('band'), may hold values from 0 to 1279, each once
- wn_ids: int32 [128], P('band'), may hold values from 0 to 1279, as said below
Outputs:
- new_grid: bfloat16 [2, 4, 1280, 2, 5248], P(None, 'fld', 'band')
Inputs may be any that keep to these rules, and one draw needn't show every extreme that they name: Latitude i has 20 + 4 i points or up to 8 fewer, a multiple of 4, never under 20; the last latitude has exactly the most. `lat_ids`: each hemispheric latitude stands in exactly one slot. `wn_ids`: distinct wavenumbers; 0 and 1279 are always among them.
All inputs are finite; a program needn't handle non-finite values.
Results may differ from a plain program's by a relative error of at most 0.014.
Values may be sent and summed in bfloat16 or wider, within the bound.
No kernel may reach another device: no remote copies, remote signals or barrier semaphores. Data moves between devices by JAX's collectives and lax.ppermute only.
A program may use at most 128 MiB of HBM per device.

v0:
```python
import math
import jax
import jax.numpy as jnp
from jax import lax
from jax.sharding import PartitionSpec as P

NT = 1279
NH = 1280
PPAD = 5248
rescale_limit = 2.0**60
rescale_log = 60.0 * math.log(2.0)


def carried_in(array, axis, join, neutral):
    place = lax.axis_index(axis)
    gathered = lax.all_gather(array.astype(jnp.bfloat16), axis)
    state = jnp.zeros_like(array) + jnp.asarray(neutral, array.dtype)

    def one(step, state):
        return join(state, lax.dynamic_index_in_dim(gathered, step, 0, False).astype(array.dtype))

    return lax.fori_loop(0, place, one, state)


def latitude_angles(lat_index):
    colatitude = math.pi * (lat_index.astype(jnp.float32) + 0.5) / (2.0 * NH)
    return (jnp.cos(colatitude), jnp.sin(colatitude))


def damping(orders):
    row_index = jnp.arange(NT + 1).astype(jnp.float32).reshape((NT + 1) // 2, 2)
    degree = row_index[:, :, None] + orders.astype(jnp.float32)[None, None, :]
    return 1.0 / (1.0 + 4.0 * degree * (degree + 1.0) / (NT * (NT + 1.0)))


def legendre_rows(orders, cosines, sines):
    order_f = orders.astype(jnp.float32)[:, None]
    step_index = jnp.arange(1, NT + 1).astype(jnp.float32)
    log_terms = jnp.log1p(0.5 / step_index)
    log_norm = 0.5 * math.log(0.5) + 0.5 * jnp.sum(
        jnp.where(step_index[None, :] <= order_f, log_terms[None, :], 0.0), axis=1
    )
    scaled_log = log_norm[:, None] + order_f * jnp.log(sines)[None, :]
    start_row = jnp.ones(scaled_log.shape, jnp.float32)
    cosine_row = cosines[None, :]
    offsets = jnp.arange(1, NT + 2).astype(jnp.float32)[:, None, None]
    degrees = order_f[None] + offsets
    factors = jnp.sqrt(
        (4.0 * degrees * degrees - 1.0) / (offsets * (2.0 * order_f[None] + offsets))
    )
    backwards = jnp.sqrt(
        (offsets - 1.0)
        * (2.0 * order_f[None] + offsets - 1.0)
        / (4.0 * (degrees - 1.0) * (degrees - 1.0) - 1.0)
    )
    inside_rows = degrees - 1.0 <= NT

    def advance(state_now, step_terms):
        current, previous, running_log = state_now
        factor, backward, inside = step_terms
        row_value = jnp.where(inside, current * jnp.exp(running_log), 0.0).astype(jnp.bfloat16)
        newest = factor * (cosine_row * current - backward * previous)
        oversize = jnp.abs(newest) > rescale_limit
        shrink = jnp.where(oversize, 1.0 / rescale_limit, 1.0)
        running_log = running_log + jnp.where(oversize, rescale_log, 0.0)
        newest = newest * shrink
        current = current * shrink
        return ((newest, current, running_log), row_value)

    final_state, every_row = lax.scan(
        advance,
        (start_row, jnp.zeros_like(start_row), scaled_log),
        (factors, backwards, inside_rows),
        unroll=8,
    )
    return every_row.reshape(((NT + 1) // 2, 2) + every_row.shape[1:])


def fourier_tables(counts, orders, blocks):
    inner_index = jnp.arange(128)
    block_start = jnp.arange(blocks) * 128
    periods = counts[:, None, None]
    inner_residue = inner_index[None, :, None] * orders[None, None, :] % periods
    block_residue = block_start[None, :, None] * orders[None, None, :] % periods
    period_f = periods.astype(jnp.float32)
    inner_angle = 2.0 * math.pi * inner_residue.astype(jnp.float32) / period_f
    block_angle = 2.0 * math.pi * block_residue.astype(jnp.float32) / period_f
    return (
        jnp.cos(inner_angle).astype(jnp.bfloat16),
        jnp.sin(inner_angle).astype(jnp.bfloat16),
        jnp.cos(block_angle),
        jnp.sin(block_angle),
    )


def analyse(grid_field, counts, orders, weights):
    blocks = PPAD // 128
    order_count = orders.shape[0]
    cos_inner, sin_inner, cos_outer, sin_outer = fourier_tables(counts, orders, blocks)
    inside = jnp.arange(PPAD)[None, :] < counts[:, None]
    masked = jnp.where(inside[:, None, :], grid_field, jnp.zeros((), jnp.bfloat16))
    shaped = masked.reshape(grid_field.shape[:-1] + (blocks, 128))
    dft_table = jnp.concatenate([cos_inner, -sin_inner], axis=-1)
    partial_sums = jnp.einsum(
        "vlshbk,skc->vlshbc", shaped, dft_table, preferred_element_type=jnp.float32
    )
    real_sums = partial_sums[..., :order_count]
    imag_sums = partial_sums[..., order_count:]
    outer_cos = cos_outer[:, None]
    outer_sin = sin_outer[:, None]
    period_f = counts.astype(jnp.float32)[:, None, None]
    real_coef = jnp.sum(outer_cos * real_sums + outer_sin * imag_sums, axis=-2) / period_f
    imag_coef = jnp.sum(outer_cos * imag_sums - outer_sin * real_sums, axis=-2) / period_f
    kept_mask = (2 * orders[None, :] < counts[:, None])[:, None, :]
    real_coef = jnp.where(kept_mask, real_coef, 0.0)
    imag_coef = jnp.where(kept_mask, imag_coef, 0.0)
    even_real = real_coef[:, :, :, 0] + real_coef[:, :, :, 1]
    even_imag = imag_coef[:, :, :, 0] + imag_coef[:, :, :, 1]
    odd_real = real_coef[:, :, :, 0] - real_coef[:, :, :, 1]
    odd_imag = imag_coef[:, :, :, 0] - imag_coef[:, :, :, 1]
    stacked = jnp.stack(
        [jnp.stack([even_real, even_imag], 2), jnp.stack([odd_real, odd_imag], 2)], 2
    )
    rounded = (weights[:, None] * stacked).astype(jnp.bfloat16)
    return jnp.swapaxes(rounded, 4, 5)


def synthesise(fourier_rows, counts, orders):
    fourier = jnp.swapaxes(fourier_rows, 4, 5)
    blocks = PPAD // 128
    cos_inner, sin_inner, cos_outer, sin_outer = fourier_tables(counts, orders, blocks)
    even_parts = fourier[:, :, 0].astype(jnp.float32)
    odd_parts = fourier[:, :, 1].astype(jnp.float32)
    hemispheres = jnp.stack([even_parts + odd_parts, even_parts - odd_parts], axis=3)
    kept_mask = 2 * orders[None, :] < counts[:, None]
    factor = jnp.where(orders == 0, 1.0, 2.0)
    hemispheres = jnp.where(kept_mask, hemispheres, 0.0) * factor
    real_hemisphere = jnp.moveaxis(hemispheres[:, :, 0], 3, 2)[..., None, :]
    imag_hemisphere = jnp.moveaxis(hemispheres[:, :, 1], 3, 2)[..., None, :]
    outer_cos = cos_outer[:, None]
    outer_sin = sin_outer[:, None]
    real_phase = outer_cos * real_hemisphere - outer_sin * imag_hemisphere
    imag_phase = outer_sin * real_hemisphere + outer_cos * imag_hemisphere
    stacked = jnp.concatenate([real_phase, imag_phase], axis=-1).astype(jnp.bfloat16)
    dft_table = jnp.concatenate([cos_inner, -sin_inner], axis=-1)
    values = jnp.einsum(
        "vlshbc,skc->vlshbk", stacked, dft_table, preferred_element_type=jnp.float32
    )
    flattened = values.reshape(values.shape[:4] + (PPAD,))
    inside = jnp.arange(PPAD)[None, :] < counts[:, None]
    return jnp.where(inside[:, None, :], flattened, 0.0).astype(jnp.bfloat16)


def add_terms(earlier, later):
    return earlier + later


def on_device(grid_field, coupling, points, lat_ids, wn_ids):
    orders, all_slots = (
        lax.all_gather(wn_ids, "band", axis=0, tiled=True),
        lax.all_gather(lat_ids, "band", axis=0, tiled=True),
    )
    counts = jnp.take(points, lat_ids)
    local_cos, local_sin = latitude_angles(lat_ids)
    weights = math.pi / (2.0 * NH) * local_sin
    coeffs = analyse(grid_field, counts, orders, weights)
    received = lax.all_to_all(coeffs, "band", split_axis=4, concat_axis=5, tiled=True)
    all_cos, all_sin = latitude_angles(all_slots)
    legendre_table = legendre_rows(wn_ids, all_cos, all_sin)
    spectral = jnp.einsum(
        "vlprmi,qpmi->vlprmq", received, legendre_table, preferred_element_type=jnp.float32
    )
    weighted = coupling[:, :, None, None, None, None] * spectral
    running = jnp.cumsum(weighted, axis=1)
    level_total = running[:, -1]
    earlier = carried_in(level_total, "fld", add_terms, jnp.zeros_like(level_total))
    damping_rows = jnp.transpose(damping(wn_ids), (1, 2, 0))[None, None, :, None, :, :]
    updated = (damping_rows * (spectral + earlier[:, None] + running - weighted)).astype(
        jnp.bfloat16
    )
    outgoing = jnp.einsum(
        "vlprmq,qpmi->vlprmi", updated, legendre_table, preferred_element_type=jnp.float32
    ).astype(jnp.bfloat16)
    fourier = lax.all_to_all(outgoing, "band", split_axis=5, concat_axis=4, tiled=True)
    return synthesise(fourier, counts, orders)


def solution(mesh):
    in_specs = (P(None, "fld", "band", None, None), P(None, "fld"), P(), P("band"), P("band"))
    out_specs = P(None, "fld", "band", None, None)
    return jax.shard_map(
        on_device, mesh=mesh, in_specs=in_specs, out_specs=out_specs, check_vma=False
    )
```

profile of v0, /device:TPU:0, one launch (start us, length us, event | category | flops | bytes accessed | tf_op | source)
XLA Modules:
  0.0 945.1 jit_solution(17061320564376272332)
XLA Ops:
  0.7 1.1 gather_fusion
  2.6 1.2 dynamic-slice
  6.8 14.1 %all-reduce.2 = (s32[1280]{0:T(1024)S(1)}, s32[128]{0:T(128)S(1)}) all-reduce(s32[1280]{0:T(1024)S(1)} %dynamic-update-slice.1, s32[128]{0:T(128)S(1)} %dynamic-update-slice), channel_id=1, replica_groups=mesh['band'=16,'fld'=2] {'band'}, use_global_device_ids=true, to_apply=%add.1 | all-reduce | flops 1408 | bytes 11264
  21.0 68.9 %cosine_convert_fusion = bf16[80,128,128]{2,1,0:T(8,128)(2,1)} fusion(f32[80]{0:T(128)S(1)} %convert_element_type.160, pred[80]{0:T(512)(128)(4,1)S(1)} %compare_bitcast_fusion, s32[80]{0:T(128)S(1)} %get-tuple-element.179, s32[128,128]{1,0:T(8,128)S(1)} %multiply_bitcast_fusion), kind=kLoop, calls=%fused_computation.156 | loop fusion | flops 14417920 | bytes 2687696 | tf_op jit(solution)/shard_map/convert_element_type | solution.py:89
  89.8 69.3 %fusion.73 = bf16[80,128,128]{2,1,0:T(8,128)(2,1)} fusion(f32[80]{0:T(128)S(1)} %convert_element_type.160, pred[80]{0:T(512)(128)(4,1)S(1)} %compare_bitcast_fusion, s32[80]{0:T(128)S(1)} %get-tuple-element.179, s32[128,128]{1,0:T(8,128)S(1)} %multiply_bitcast_fusion), kind=kLoop, calls=%fused_computation.163 | loop fusion | flops 18350080 | bytes 2687696 | tf_op jit(solution)/shard_map/neg | solution.py:145
  159.5 7.6 copy_select_fusion.1
  167.1 11.7 %reshape.556 = bf16[2,2,80,2,41,128]{5,4,2,3,1,0:T(8,128)(2,1)} reshape(bf16[2,2,80,2,5248]{4,2,3,1,0:T(8,128)(2,1)} %copy_select_fusion.1) | data formatting | bytes 13434880 | tf_op jit(solution)/shard_map/reshape | solution.py:102
  178.9 27.8 %fusion.90 = (f32[80,41,128]{2,1,0:T(8,128)S(1)}, f32[80,41,128]{2,1,0:T(8,128)}) fusion(f32[80]{0:T(128)S(1)} %convert_element_type.160, pred[80]{0:T(512)(128)(4,1)S(1)} %compare_bitcast_fusion, s32[80]{0:T(128)S(1)} %get-tuple-element.179, s32[41,128]{1,0:T(8,128)S(1)} %multiply_bitcast_fusion.1), kind=kLoop, calls=%fused_computation.176 | loop fusion | flops 4198400 | bytes 3380432 | tf_op jit(solution)/shard_map/cos | solution.py:91
  206.8 15.3 %convolution_bitcast_fusion = f32[2,2,80,2,41,256]{5,4,3,1,0,2:T(8,128)} fusion(bf16[2,2,80,2,41,128]{5,4,2,3,1,0:T(8,128)(2,1)} %reshape.556, bf16[80,128,128]{2,1,0:T(8,128)(2,1)} %fusion.73, bf16[80,128,128]{2,1,0:T(8,128)(2,1)} %cosine_convert_fusion), kind=kOutput, calls=%fused_computation.143 | convolution fusion | flops 1730150400 | bytes 38830080 | tf_op jit(solution)/shard_map/vlshbk,skc->vlshbc/dot_general | solution.py:104
  222.1 13.3 %add_reduce_fusion = (f32[2,2,80,2,128]{4,3,1,0,2:T(2,128)S(1)}, f32[2,2,80,2,128]{4,3,1,0,2:T(2,128)S(1)}) fusion(f32[2,2,80,2,41,256]{5,4,3,1,0,2:T(8,128)} %convolution_bitcast_fusion, f32[80,41,128]{2,1,0:T(8,128)} %get-tuple-element.226, f32[80,41,128]{2,1,0:T(8,128)S(1)} %get-tuple-element.225), kind=kLoop, calls=%fused_computation.140 | loop fusion | flops 26705920 | bytes 30883840 | tf_op jit(solution)/shard_map/reduce_sum | solution.py:112
  237.1 2.0 copy.124
  239.1 3.7 all-to-all-start
  243.4 1.1 copy.112
  245.6 2.0 copy.114
  247.6 524.3 %while.28 = (s32[]{:T(128)}, f32[8,1280]{1,0:T(8,128)S(1)}, f32[8,1280]{1,0:T(8,128)S(1)}, f32[8,1280]{1,0:T(8,128)S(1)}, bf16[160,8,8,1280]{3,2,1,0:T(8,128)(2,...) while((s32[]{:T(128)}, f32[8,1280]{1,0:T(8,128)S(1)}, ...), condition=%wide.region_2.5_spmd.clone, body=%wide.region_1.4_spmd.clone.sunk | while | flops 2754569 | bytes 1978075 | solution.py:70
  772.3 1.6 all_to_all.29
  773.9 22.5 %fusion.85 = f32[2,2,2,2,8,640]{5,3,1,0,4,2:T(2,128)S(1)} fusion(bf16[2,2,2,2,8,1280]{5,3,1,0,4,2:T(2,128)(2,1)} %all_to_all.29, bf16[640,2,8,1280,1,1]{3,2,1,0,5,4:T(8,128)(2,1)} %bitcast.216), kind=kOutput, calls=%fused_computation.172 | convolution fusion | flops 209715200 | bytes 26869760 | tf_op jit(solution)/shard_map/vlprmi,qpmi->vlprmq/dot_general | solution.py:170
  796.7 5.4 all-gather
  802.2 18.4 %fusion.77 = bf16[2,2,2,2,8,1280]{5,3,1,0,4,2:T(2,128)(2,1)} fusion(bf16[640,2,8,1280,1,1]{3,2,1,0,5,4:T(8,128)(2,1)} %bitcast.217, f32[2,2,2,2,8,640]{5,3,1,0,4,2:T(2,128)S(1)} %fusion.96, f32[2,2,2,2,8,640]{5,3,1,0,4,2:T(2,128)S(1)} %fusion.85, f32[2,2,2,8,640]{4,2,0,3,1:T(2,128)S(1)} %copy.129, f32[2,2]{1,0:T(2,128)S(1)} %copy-done.2, ...), kind=kOutput, calls=%fused_computation.165 | convolution fusion | flops 210370560 | bytes 27402256 | tf_op jit(solution)/shard_map/vlprmq,qpmi->vlprmi/dot_general | solution.py:181
  820.6 10.4 %copy.131 = bf16[2,2,2,2,8,1280]{4,3,2,1,0,5:T(2,128)(2,1)} copy(bf16[2,2,2,2,8,1280]{5,3,1,0,4,2:T(2,128)(2,1)} %fusion.77) | data formatting | bytes 655360 | tf_op jit(solution)/shard_map/convert_element_type | solution.py:183
  831.0 15.5 %reshape.584 = bf16[16,2,5120]{2,1,0:T(2,128)(2,1)} reshape(bf16[1280,2,2,2,2,8]{5,4,3,2,1,0:T(2,128)(2,1)} %bitcast.206) | data formatting | bytes 655360
  846.5 6.1 all-to-all-start.1
  852.7 10.9 %all-to-all-done.1 = bf16[16,2,5120]{2,1,0:T(2,128)(2,1)S(1)} async-done(((bf16[16,2,5120]{2,1,0:T(2,128)(2,1)}), bf16[16,2,5120]{2,1,0:T(2,128)(2,1)S(1)}, u32[]{:S(2)}, u32[]{:S(2)}) %all-to-all-start.1) | async-done | bytes 327712 | tf_op jit(solution)/shard_map/all_to_all | solution.py:184
  863.6 7.2 reshape.585
  870.8 9.5 %copy.132 = bf16[2,2,2,2,8,16,80]{6,4,5,3,2,1,0:T(8,128)(2,1)S(1)} copy(bf16[2,2,2,2,8,16,80]{4,3,2,1,0,6,5:T(2,128)(2,1)} %bitcast.204) | data formatting | bytes 655360 | tf_op jit(solution)/shard_map/all_to_all | solution.py:184
  880.3 10.6 %copy.147 = bf16[2,2,2,2,8,16,80]{6,4,5,3,1,0,2:T(8,128)(2,1)} copy(bf16[2,2,2,2,8,16,80]{4,3,2,1,0,6,5:T(2,128)(2,1)} %bitcast.205) | data formatting | bytes 655360 | tf_op jit(solution)/shard_map/transpose | solution.py:129
  894.0 1.3 copy.136
  896.2 8.6 subtract_convert_fusion
  904.8 11.2 %fusion.64 = bf16[2,2,80,2,41,128]{5,4,3,1,0,2:T(8,128)(2,1)} fusion(bf16[2,2,80,2,41,128]{5,4,3,1,0,2:T(8,128)(2,1)} %get-tuple-element.217, bf16[2,2,80,2,41,128]{5,4,3,1,0,2:T(8,128)(2,1)} %get-tuple-element.216, bf16[80,128,128]{2,1,0:T(8,128)(2,1)} %fusion.73, bf16[80,128,128]{2,1,0:T(8,128)(2,1)} %cosine_convert_fusion), kind=kOutput, calls=%fused_computation.148 | convolution fusion | flops 1757020160 | bytes 25395200 | tf_op jit(solution)/shard_map/vlshbc,skc->vlshbk/dot_general | solution.py:146
  916.0 14.4 %reshape.582 = bf16[2,2,80,2,5248]{4,3,1,0,2:T(2,128)(2,1)} reshape(bf16[2,2,80,2,41,128]{5,4,3,1,0,2:T(8,128)(2,1)} %fusion.64) | data formatting | bytes 13434880 | tf_op jit(solution)/shard_map/reshape | solution.py:149
  930.5 4.1 fusion.63
  934.6 10.1 %copy.139 = bf16[2,2,80,2,5248]{4,3,2,1,0:T(2,128)(2,1)} copy(bf16[2,2,80,2,5248]{4,2,3,1,0:T(8,128)(2,1)S(1)} %fusion.63) | data formatting | bytes 13434880 | tf_op jit(solution)/shard_map/convert_element_type | solution.py:151
  (2147 shorter events, 527.9 us)
Async XLA Ops:
  0.0 0.7 copy-start
  0.0 159.5 %copy-start.3 = (s32[80]{0:T(128)S(1)}, s32[80]{0:T(128)}, u32[]{:S(2)}) copy-start(s32[80]{0:T(128)} %param.16) | copy-start | bytes 964
  235.4 7.4 copy-start.4
  239.1 533.0 %all-to-all-start = ((bf16[2,2,2,2,128,80]{5,3,2,1,0,4:T(2,128)(2,1)}), bf16[2,2,2,2,128,80]{5,3,2,1,0,4:T(2,128)(2,1)S(1)}, u32[]{:S(2)}, u32[]{:S(2)}) async-start(bf16[2,2,2,2,128,80]{5,3,2,1,0,4:T(2,128)(2,1)} %copy.124), calls=%async_computation | async-start | bytes 1048576 | tf_op jit(solution)/shard_map/all_to_all | solution.py:167
  773.9 22.6 %copy-start.2 = (f32[2,2]{1,0:T(2,128)S(1)}, f32[2,2]{1,0:T(2,128)}, u32[]{:S(2)}) copy-start(f32[2,2]{1,0:T(2,128)} %param.14) | copy-start | bytes 52
  846.5 17.1 %all-to-all-start.1 = ((bf16[16,2,5120]{2,1,0:T(2,128)(2,1)}), bf16[16,2,5120]{2,1,0:T(2,128)(2,1)S(1)}, u32[]{:S(2)}, u32[]{:S(2)}) async-start(bf16[16,2,5120]{2,1,0:T(2,128)(2,1)} %reshape.584), calls=%async_computation.1 | async-start | bytes 655360 | tf_op jit(solution)/shard_map/all_to_all | solution.py:184
  930.4 14.2 %copy-start.1 = (s32[1280]{0:T(1024)S(1)}, s32[1280]{0:T(1024)}, u32[]{:S(2)}) copy-start(s32[1280]{0:T(1024)} %param.15) | copy-start | bytes 15364
where the time goes:
time: 957 us; the launch traced here: 945 us
  local copies, waits for them, and re-layouts  458 us (48%)
  other arithmetic  370 us (39%)
  matrix products  67.4 us (7%)
  blocking collectives  19.5 us (2%)
  waiting for transfers between devices  10.9 us (1%)
  starting transfers between devices  9.8 us (1%)
    mul x160, local copies, waits for them, and re-layouts, advance(): newest = factor * (cosine_row * current - backward * previous)  128 us
    while x1120, other arithmetic  119 us
    broadcast_in_dim x160, local copies, waits for them, and re-layouts, advance(): jnp.where(inside, current * jnp.exp(running_log), 0.0).astype(jnp.bfloat16)  115 us
    dynamic_update_slice x160, local copies, waits for them, and re-layouts, legendre_rows(): lax.scan(advance, (start_row, jnp.zeros_like(start_row), scaled_log), (fa...  109 us
    neg x1, other arithmetic, synthesise(): dft_table = jnp.concatenate([cos_inner, -sin_inner], axis=-1)  69.3 us
    convert_element_type x1, other arithmetic, fourier_tables(): jnp.cos(inner_angle).astype(jnp.bfloat16)  68.9 us
    unnamed x20, local copies, waits for them, and re-layouts  29.8 us
    cos x1, other arithmetic, fourier_tables(): jnp.cos(block_angle)  27.8 us
  transfers between devices with their start and end apart: 2, of which 1 were waited for; matrix products, arithmetic and copies ran while one was open for 55% of the time, Pallas kernels for 0%

commit v1 on v0

--- a/solution.py
+++ b/solution.py
@@ -9,6 +9,16 @@
 PPAD = 5248
 rescale_limit = 2.0**60
 rescale_log = 60.0 * math.log(2.0)
+
+
+def get_rates(inner_x):
+    found_now = lax.all_to_all(
+        jnp.stack(jnp.split(inner_x, lax.axis_size("band"), axis=5)),
+        "band",
+        split_axis=0,
+        concat_axis=0,
+    )
+    return jnp.concatenate(found_now, axis=4)
 
 
 def carried_in(array, axis, join, neutral):
@@ -181,7 +191,7 @@
     outgoing = jnp.einsum(
         "vlprmq,qpmi->vlprmi", updated, legendre_table, preferred_element_type=jnp.float32
     ).astype(jnp.bfloat16)
-    fourier = lax.all_to_all(outgoing, "band", split_axis=5, concat_axis=4, tiled=True)
+    fourier = get_rates(outgoing)
     return synthesise(fourier, counts, orders)
 
 

time: 957 us -> 908 us (0.949)
  local copies, waits for them, and re-layouts: 458 us -> 404 us
    unnamed x20 -> x35, local copies, waits for them, and re-layouts: 29.8 us -> 18.1 us
    transpose x1, local copies, waits for them, and re-layouts: 10.6 us -> 0.1 us  [synthesise(): fourier = jnp.swapaxes(fourier_rows, 4, 5)]
    convert_element_type x1 -> x0, local copies, waits for them, and re-layouts: 10.4 us -> none  [on_device(): outgoing = jnp.einsum('vlprmq,qpmi->vlprmi', updated, legendre_table, pre...]
  transfers between devices with their start and end apart: 2 -> 2, of which waited for: 1 -> 1; matrix products, arithmetic and copies ran while one was open for 55% -> 57% of each run, Pallas kernels for 0% -> 0%
where the time goes in v1:
time: 908 us; the launch traced here: 897 us
  local copies, waits for them, and re-layouts  404 us (44%)
  other arithmetic  368 us (41%)
  matrix products  71.7 us (8%)
  blocking collectives  19.5 us (2%)
  waiting for transfers between devices  14.1 us (2%)
  starting transfers between devices  9.81 us (1%)
    while x1120, other arithmetic  119 us
    mul x160, local copies, waits for them, and re-layouts, advance(): newest = factor * (cosine_row * current - backward * previous)  119 us
    broadcast_in_dim x160, local copies, waits for them, and re-layouts, advance(): jnp.where(inside, current * jnp.exp(running_log), 0.0).astype(jnp.bfloat16)  115 us
    dynamic_update_slice x160, local copies, waits for them, and re-layouts, legendre_rows(): lax.scan(advance, (start_row, jnp.zeros_like(start_row), scaled_log), (fa...  109 us
    neg x1, other arithmetic, synthesise(): dft_table = jnp.concatenate([cos_inner, -sin_inner], axis=-1)  69.4 us
    convert_element_type x1, other arithmetic, fourier_tables(): jnp.cos(inner_angle).astype(jnp.bfloat16)  68.9 us
    cos x1, other arithmetic, fourier_tables(): jnp.cos(block_angle)  27.8 us
    dot_general x1, matrix products, on_device(): jnp.einsum('vlprmq,qpmi->vlprmi', updated, legendre_table, preferred_elem...  22.7 us
  transfers between devices with their start and end apart: 2, of which 1 were waited for; matrix products, arithmetic and copies ran while one was open for 57% of the time, Pallas kernels for 0%

profile of v1, /device:TPU:0, one launch (start us, length us, event | category | flops | bytes accessed | tf_op | source)
XLA Modules:
  0.0 897.1 jit_solution(575597854247605540)
XLA Ops:
  0.7 1.1 gather_fusion
  2.6 1.2 dynamic-slice
  5.1 0.9 dynamic-update-slice.1
  6.0 0.8 dynamic-update-slice
  6.8 14.1 %all-reduce.2 = (s32[1280]{0:T(1024)S(1)}, s32[128]{0:T(128)S(1)}) all-reduce(s32[1280]{0:T(1024)S(1)} %dynamic-update-slice.1, s32[128]{0:T(128)S(1)} %dynamic-update-slice), channel_id=1, replica_groups=mesh['band'=16,'fld'=2] {'band'}, use_global_device_ids=true, to_apply=%add.1 | all-reduce | flops 1408 | bytes 11264
  21.0 68.9 %cosine_convert_fusion = bf16[80,128,128]{2,1,0:T(8,128)(2,1)} fusion(f32[80]{0:T(128)S(1)} %convert_element_type.160, pred[80]{0:T(512)(128)(4,1)S(1)} %compare_bitcast_fusion, s32[80]{0:T(128)S(1)} %get-tuple-element.175, s32[128,128]{1,0:T(8,128)S(1)} %multiply_bitcast_fusion), kind=kLoop, calls=%fused_computation.156 | loop fusion | flops 14417920 | bytes 2687696 | tf_op jit(solution)/shard_map/convert_element_type | solution.py:99
  89.8 69.4 %fusion.73 = bf16[80,128,128]{2,1,0:T(8,128)(2,1)} fusion(f32[80]{0:T(128)S(1)} %convert_element_type.160, pred[80]{0:T(512)(128)(4,1)S(1)} %compare_bitcast_fusion, s32[80]{0:T(128)S(1)} %get-tuple-element.175, s32[128,128]{1,0:T(8,128)S(1)} %multiply_bitcast_fusion), kind=kLoop, calls=%fused_computation.163 | loop fusion | flops 18350080 | bytes 2687696 | tf_op jit(solution)/shard_map/neg | solution.py:155
  159.6 7.6 copy_select_fusion.1
  167.2 11.7 %reshape.562 = bf16[2,2,80,2,41,128]{5,4,2,3,1,0:T(8,128)(2,1)} reshape(bf16[2,2,80,2,5248]{4,2,3,1,0:T(8,128)(2,1)} %copy_select_fusion.1) | data formatting | bytes 13434880 | tf_op jit(solution)/shard_map/reshape | solution.py:112
  178.9 27.8 %fusion.90 = (f32[80,41,128]{2,1,0:T(8,128)S(1)}, f32[80,41,128]{2,1,0:T(8,128)}) fusion(f32[80]{0:T(128)S(1)} %convert_element_type.160, pred[80]{0:T(512)(128)(4,1)S(1)} %compare_bitcast_fusion, s32[80]{0:T(128)S(1)} %get-tuple-element.175, s32[41,128]{1,0:T(8,128)S(1)} %multiply_bitcast_fusion.1), kind=kLoop, calls=%fused_computation.176 | loop fusion | flops 4198400 | bytes 3380432 | tf_op jit(solution)/shard_map/cos | solution.py:101
  206.8 15.3 %convolution_bitcast_fusion = f32[2,2,80,2,41,256]{5,4,3,1,0,2:T(8,128)} fusion(bf16[2,2,80,2,41,128]{5,4,2,3,1,0:T(8,128)(2,1)} %reshape.562, bf16[80,128,128]{2,1,0:T(8,128)(2,1)} %fusion.73, bf16[80,128,128]{2,1,0:T(8,128)(2,1)} %cosine_convert_fusion), kind=kOutput, calls=%fused_computation.143 | convolution fusion | flops 1730150400 | bytes 38830080 | tf_op jit(solution)/shard_map/vlshbk,skc->vlshbc/dot_general | solution.py:114
  222.1 13.3 %add_reduce_fusion = (f32[2,2,80,2,128]{4,3,1,0,2:T(2,128)S(1)}, f32[2,2,80,2,128]{4,3,1,0,2:T(2,128)S(1)}) fusion(f32[2,2,80,2,41,256]{5,4,3,1,0,2:T(8,128)} %convolution_bitcast_fusion, f32[80,41,128]{2,1,0:T(8,128)} %get-tuple-element.222, f32[80,41,128]{2,1,0:T(8,128)S(1)} %get-tuple-element.221), kind=kLoop, calls=%fused_computation.140 | loop fusion | flops 26705920 | bytes 30883840 | tf_op jit(solution)/shard_map/reduce_sum | solution.py:122
  237.1 2.0 copy.95
  239.1 3.7 all-to-all-start
  243.4 1.1 copy.83
  244.5 1.1 copy.84
  245.6 2.0 copy.85
  247.7 513.7 %while.28 = (s32[]{:T(128)}, f32[8,1280]{1,0:T(8,128)S(1)}, f32[8,1280]{1,0:T(8,128)S(1)}, f32[8,1280]{1,0:T(8,128)S(1)}, bf16[160,8,8,1280]{3,2,1,0:T(8,128)(2,...) while((s32[]{:T(128)}, f32[8,1280]{1,0:T(8,128)S(1)}, ...), condition=%wide.region_2.5_spmd.clone, body=%wide.region_1.4_spmd.clone.sunk | while | flops 2754569 | bytes 1978075 | solution.py:80
  476.4 0.8 fusion.146
  710.7 0.8 fusion.146
  761.8 1.6 all_to_all.19
  763.3 22.5 %fusion.85 = f32[2,2,2,2,8,640]{5,3,1,0,4,2:T(2,128)S(1)} fusion(bf16[2,2,2,2,8,1280]{5,3,1,0,4,2:T(2,128)(2,1)} %all_to_all.19, bf16[640,2,8,1280,1,1]{3,2,1,0,5,4:T(8,128)(2,1)} %bitcast.279), kind=kOutput, calls=%fused_computation.172 | convolution fusion | flops 209715200 | bytes 26869760 | tf_op jit(solution)/shard_map/vlprmi,qpmi->vlprmq/dot_general | solution.py:180
  786.6 5.4 all-gather
  792.1 22.7 %fusion.77 = bf16[2,2,2,2,8,1280]{5,3,1,0,4,2:T(2,128)(2,1)S(1)} fusion(bf16[640,2,8,1280,1,1]{3,2,1,0,5,4:T(8,128)(2,1)} %bitcast.280, f32[2,2,2,2,8,640]{5,3,1,0,4,2:T(2,128)S(1)} %fusion.96, f32[2,2,2,2,8,640]{5,3,1,0,4,2:T(2,128)} %copy-done.2, f32[2,2,2,8,640]{4,2,0,3,1:T(2,128)S(1)} %copy.100, f32[2,2]{1,0:T(2,128)S(1)} %copy-done.3, ...), kind=kOutput, calls=%fused_computation.165 | convolution fusion | flops 210370560 | bytes 27402256 | tf_op jit(solution)/shard_map/vlprmq,qpmi->vlprmi/dot_general | solution.py:191
  826.0 6.1 all-to-all-start.1
  832.2 14.1 %all-to-all-done.1 = bf16[16,2,2,2,2,8,80]{6,4,2,1,5,3,0:T(2,128)(2,1)S(1)} async-done(((bf16[16,2,2,2,2,8,80]{6,4,2,1,5,3,0:T(2,128)(2,1)}), bf16[16,2,2,2,2,8,80]{6,4,2,1,5,3,0:T(2,128)(2,1)S(1)}, u32[]{:S(2)}, u32[]{:S(2)}) %all-to-all-start.1) | async-done | bytes 327712 | tf_op jit(solution)/shard_map/all_to_all | solution.py:15
  847.0 0.9 copy.106
  848.1 8.7 subtract_convert_fusion
  856.8 11.2 %fusion.64 = bf16[2,2,80,2,41,128]{5,4,3,1,0,2:T(8,128)(2,1)} fusion(bf16[2,2,80,2,41,128]{5,4,3,1,0,2:T(8,128)(2,1)} %get-tuple-element.213, bf16[2,2,80,2,41,128]{5,4,3,1,0,2:T(8,128)(2,1)} %get-tuple-element.212, bf16[80,128,128]{2,1,0:T(8,128)(2,1)} %fusion.73, bf16[80,128,128]{2,1,0:T(8,128)(2,1)} %cosine_convert_fusion), kind=kOutput, calls=%fused_computation.148 | convolution fusion | flops 1757020160 | bytes 25395200 | tf_op jit(solution)/shard_map/vlshbc,skc->vlshbk/dot_general | solution.py:156
  868.0 14.4 %reshape.590 = bf16[2,2,80,2,5248]{4,3,1,0,2:T(2,128)(2,1)} reshape(bf16[2,2,80,2,41,128]{5,4,3,1,0,2:T(8,128)(2,1)} %fusion.64) | data formatting | bytes 13434880 | tf_op jit(solution)/shard_map/reshape | solution.py:159
  882.5 4.1 fusion.63
  886.6 10.1 %copy.109 = bf16[2,2,80,2,5248]{4,3,2,1,0:T(2,128)(2,1)} copy(bf16[2,2,80,2,5248]{4,2,3,1,0:T(8,128)(2,1)S(1)} %fusion.63) | data formatting | bytes 13434880 | tf_op jit(solution)/shard_map/convert_element_type | solution.py:161
  (2162 shorter events, 521.6 us)
Async XLA Ops:
  0.0 0.7 copy-start
  0.0 159.5 %copy-start.4 = (s32[80]{0:T(128)S(1)}, s32[80]{0:T(128)}, u32[]{:S(2)}) copy-start(s32[80]{0:T(128)} %param.16) | copy-start | bytes 964
  235.4 7.4 copy-start.5
  239.1 522.4 %all-to-all-start = ((bf16[2,2,2,2,128,80]{5,3,2,1,0,4:T(2,128)(2,1)}), bf16[2,2,2,2,128,80]{5,3,2,1,0,4:T(2,128)(2,1)S(1)}, u32[]{:S(2)}, u32[]{:S(2)}) async-start(bf16[2,2,2,2,128,80]{5,3,2,1,0,4:T(2,128)(2,1)} %copy.95), calls=%async_computation | async-start | bytes 1048576 | tf_op jit(solution)/shard_map/all_to_all | solution.py:177
  763.3 22.5 %copy-start.3 = (f32[2,2]{1,0:T(2,128)S(1)}, f32[2,2]{1,0:T(2,128)}, u32[]{:S(2)}) copy-start(f32[2,2]{1,0:T(2,128)} %param.14) | copy-start | bytes 52
  785.8 0.7 copy-start.2
  826.0 20.3 %all-to-all-start.1 = ((bf16[16,2,2,2,2,8,80]{6,4,2,1,5,3,0:T(2,128)(2,1)}), bf16[16,2,2,2,2,8,80]{6,4,2,1,5,3,0:T(2,128)(2,1)S(1)}, u32[]{:S(2)}, u32[]{:S(2)}) async-start(bf16[16,2,2,2,2,8,80]{6,4,2,1,5,3,0:T(2,128)(2,1)} %fusion.116), calls=%async_computation.1 | async-start | bytes 1048576 | tf_op jit(solution)/shard_map/all_to_all | solution.py:15
  882.4 14.2 %copy-start.1 = (s32[1280]{0:T(1024)S(1)}, s32[1280]{0:T(1024)}, u32[]{:S(2)}) copy-start(s32[1280]{0:T(1024)} %param.15) | copy-start | bytes 15364
